TPU v7x, 32 devices: a whole 2x2x4 slice. The times are simulated.
32 devices in a mesh: code: 4 (over y, core), vocab: 8 (over z, x).
Axes of the slice: x: 2, y: 2, z: 4, core: 2. Of those that a mesh axis runs over, the one named last changes fastest.
Arguments:
- latent_activations: bfloat16 [512, 8192], P(None, 'vocab'), may hold values from -150 to 150
- code_fragments: bfloat16 [4, 5344, 8192], P('code', 'vocab'), may hold values from -0.25 to 0.25
- remaining_fragments: int32 [8, 2], P('vocab'), may hold values from 0 to 3, as said below
Outputs:
- log_probs: float32 [512, 10688], P('code', 'vocab')
Inputs may be any that keep to these rules, and one draw needn't show every extreme that they name: `remaining_fragments`: each row holds 2 different share numbers in increasing order.
All inputs are finite; a program needn't handle non-finite values.
Results may differ from a plain program's by a relative error of at most 0.0003.
Values may be sent and summed in bfloat16 or wider, within the bound.
A program may use at most 128 MiB of HBM per device.

v0:
```python
import jax
import jax.numpy as jnp
from jax import lax
from jax.sharding import PartitionSpec as P


def generator(count):
    nodes = jnp.cos(jnp.pi * (jnp.arange(count).astype(jnp.float32) + 0.5) / count)
    return jnp.concatenate(
        [jnp.eye(count, dtype=jnp.float32), jnp.ones((1, count), jnp.float32), nodes[None, :]],
        axis=0,
    )


def invert(matrix):
    matrix_rank_order = matrix.shape[0]
    left_part = matrix
    right_part = jnp.eye(matrix_rank_order, dtype=jnp.float32)
    taken_rows = jnp.zeros((matrix_rank_order,), jnp.float32)
    positions = jnp.arange(matrix_rank_order)
    for column in range(matrix_rank_order):
        scores = jnp.where(taken_rows > 0, -1.0, jnp.abs(left_part[:, column]))
        chosen = (positions == jnp.argmax(scores)).astype(jnp.float32)
        pivot_left = jnp.dot(chosen, left_part, precision=lax.Precision.HIGHEST)
        pivot_right = jnp.dot(chosen, right_part, precision=lax.Precision.HIGHEST)
        pivot_value = pivot_left[column]
        pivot_left = pivot_left / pivot_value
        pivot_right = pivot_right / pivot_value
        factors = left_part[:, column] * (1.0 - chosen)
        keep_rows = (1.0 - chosen)[:, None]
        left_part = (left_part - factors[:, None] * pivot_left[None, :]) * keep_rows + chosen[
            :, None
        ] * pivot_left[None, :]
        right_part = (right_part - factors[:, None] * pivot_right[None, :]) * keep_rows + chosen[
            :, None
        ] * pivot_right[None, :]
        taken_rows = taken_rows + chosen
    return jnp.dot(left_part.T, right_part, precision=lax.Precision.HIGHEST)


def restoring_operator(chosen_row, fragment_count):
    data_count = chosen_row.shape[0]
    select = (chosen_row[:, None] == jnp.arange(fragment_count)[None, :]).astype(jnp.float32)
    square = jnp.dot(select, generator(data_count), precision=lax.Precision.HIGHEST)
    return jnp.dot(invert(square), select, precision=lax.Precision.HIGHEST)


def shards(latent_activations, code_fragments, remaining_fragments):
    local_rows = code_fragments[0]
    fragment_count = lax.axis_size("code")
    encoded = lax.dot_general(
        lax.all_gather(latent_activations, "vocab", axis=1, tiled=True),
        local_rows,
        (((1,), (1,)), ((), ())),
        preferred_element_type=jnp.float32,
    )
    restored_lines = restoring_operator(remaining_fragments[0], fragment_count)
    rows_own = encoded.shape[0] // fragment_count
    split_rows = encoded.reshape(fragment_count, rows_own, encoded.shape[1])
    payload_rows = jnp.einsum(
        "hg,giu->ihu",
        restored_lines,
        lax.all_to_all(split_rows, "code", split_axis=0, concat_axis=0, tiled=True),
        precision=lax.Precision.HIGHEST,
    )
    logits = payload_rows.reshape(
        payload_rows.shape[0], payload_rows.shape[1] * payload_rows.shape[2]
    )
    local_top = jnp.max(logits, axis=1)
    top = lax.pmax(local_top, "vocab")
    total = lax.psum(jnp.sum(jnp.exp(logits - top[:, None]), axis=1), "vocab")
    normalizer = top + jnp.log(total)
    return logits - normalizer[:, None]


def solution(mesh):
    return jax.shard_map(
        shards,
        mesh=mesh,
        in_specs=(P(None, "vocab"), P("code", "vocab", None), P("vocab", None)),
        out_specs=P("code", "vocab"),
        check_vma=False,
    )
```

profile of v0, /device:TPU:0, one launch (start us, length us, event | category | flops | bytes accessed | tf_op | source)
XLA Modules:
  0.0 217.8 jit_solution(18337576836306643534)
XLA Ops:
  6.5 0.7 all-gather.2.cloned.1.call-update
  7.4 0.8 fusion.6
  8.4 0.7 iota_reduce_fusion
  9.6 0.7 convolution_bitcast_fusion.4
  10.3 0.7 fusion.5
  11.0 0.7 fusion.17
  11.7 0.6 broadcast_subtract_fusion.2
  12.5 1.3 fusion.24
  13.8 0.8 convolution_bitcast_fusion.3
  14.7 122.1 %all-gather.2.cloned.1.call-done = bf16[512,8192]{1,0:T(8,128)(2,1)} async-done(((bf16[512,1024]{1,0:T(8,128)(2,1)}), bf16[512,8192]{1,0:T(8,128)(2,1)}) %all-gather.2.cloned.1.call-update) | async-done | bytes 8388624 | tf_op jit(solution)/shard_map/all_gather | solution.py:52
  136.7 11.1 %fusion = f32[4,128,668]{1,2,0:T(8,128)} fusion(bf16[4,128,8192]{2,1,0:T(8,128)(2,1)} %bitcast.48, bf16[1,668,8192]{2,1,0:T(8,128)(2,1)} %param.4), kind=kOutput, calls=%fused_computation | convolution fusion | flops 5603590144 | bytes 20701184 | tf_op jit(solution)/shard_map/dot_general | solution.py:51
  147.8 3.5 %all-to-all-start = ((f32[4,128,668]{1,2,0:T(8,128)}), f32[4,128,668]{1,2,0:T(8,128)S(1)}, u32[]{:S(2)}, u32[]{:S(2)}) async-start(f32[4,128,668]{1,2,0:T(8,128)} %fusion), calls=%async_computation | async-start | bytes 2752512 | tf_op jit(solution)/shard_map/all_to_all | solution.py:63
  151.4 0.7 broadcast_subtract_fusion.1
  152.1 0.6 slice.17
  152.7 0.7 fusion.28
  153.4 0.9 fusion.20
  154.2 0.7 broadcast_divide_fusion
  154.9 1.5 fusion.4
  156.9 12.4 %all-to-all-done = f32[4,128,668]{1,2,0:T(8,128)S(1)} async-done(((f32[4,128,668]{1,2,0:T(8,128)}), f32[4,128,668]{1,2,0:T(8,128)S(1)}, u32[]{:S(2)}, u32[]{:S(2)}) %all-to-all-start) | async-done | bytes 1368096 | tf_op jit(solution)/shard_map/all_to_all | solution.py:63
  169.3 3.6 %fusion.39 = (f32[128]{0:T(128)S(1)}, f32[128,668,2]{0,2,1:T(2,128)S(1)}) fusion(f32[2,4,1]{1,0,2:T(2,128)S(1)} %convolution_bitcast_fusion, f32[4,128,668]{1,2,0:T(8,128)S(1)} %all-to-all-done), kind=kOutput, calls=%fused_computation.66 | convolution fusion | flops 8379264 | bytes 2052640 | tf_op jit(solution)/shard_map/hg,giu->ihu/dot_general | solution.py:60
  172.9 18.5 %pmax.7 = f32[128]{0:T(128)S(1)} all-reduce(f32[128]{0:T(128)S(1)} %get-tuple-element.9), channel_id=1, replica_groups=mesh['code'=4,'vocab'=8] {'vocab'}, use_global_device_ids=true, to_apply=%region_3.4 | all-reduce | flops 128 | bytes 1024 | tf_op jit(solution)/shard_map/pmax | solution.py:70
  191.4 0.7 exponential_reduce_fusion
  192.2 17.8 %psum.7 = f32[128]{0:T(128)S(1)} all-reduce(f32[128]{0:T(128)S(1)} %exponential_reduce_fusion), channel_id=1, replica_groups=mesh['code'=4,'vocab'=8] {'vocab'}, use_global_device_ids=true, to_apply=%region_5.6 | all-reduce | flops 128 | bytes 1024 | tf_op jit(solution)/shard_map/psum | solution.py:71
  210.0 0.9 broadcast_subtract_fusion
  (15 shorter events, 1.6 us)
Async XLA Ops:
  6.5 130.2 %all-gather.2.cloned.1.call-start = ((), (), s32[]{:S(2)}) async-start(), calls=%async_computation.1 | async-start | bytes 9437184 | tf_op jit(solution)/shard_map/all_gather | solution.py:52
  136.7 20.0 %copy-start = (s32[1,2]{1,0:T(1,128)S(1)}, s32[1,2]{1,0:T(1,128)}, u32[]{:S(2)}) copy-start(s32[1,2]{1,0:T(1,128)} %param.5) | copy-start | bytes 28
  147.8 21.5 %all-to-all-start = ((f32[4,128,668]{1,2,0:T(8,128)}), f32[4,128,668]{1,2,0:T(8,128)S(1)}, u32[]{:S(2)}, u32[]{:S(2)}) async-start(f32[4,128,668]{1,2,0:T(8,128)} %fusion), calls=%async_computation | async-start | bytes 2752512 | tf_op jit(solution)/shard_map/all_to_all | solution.py:63
Sparse Core Ops, SparseCore 0:
  9.5 127.1 all-gather.1
where the time goes:
time: 218 us
  waiting for transfers between devices  135 us (62%)
  blocking collectives  36.3 us (17%)
  matrix products  19.8 us (9%)
  between operations  13.5 us (6%)
  other arithmetic  8.74 us (4%)
  starting transfers between devices  3.55 us (2%)
    all_gather x1, waiting for transfers between devices, shards(): lax.all_gather(latent_activations, 'vocab', axis=1, tiled=True)  122 us
    pmax x1, blocking collectives, shards(): top = lax.pmax(local_top, 'vocab')  18.5 us
    psum x1, blocking collectives, shards(): total = lax.psum(jnp.sum(jnp.exp(logits - top[:, None]), axis=1), 'vocab')  17.8 us
    all_to_all x1, waiting for transfers between devices, shards(): lax.all_to_all(split_rows, 'code', split_axis=0, concat_axis=0, tiled=True)  12.4 us
    dot_general x1, matrix products, shards(): lax.dot_general(lax.all_gather(latent_activations, 'vocab', axis=1, tiled...  11.1 us
  transfers between devices with their start and end apart: 2, of which 2 were waited for; matrix products, arithmetic and copies ran while one was open for 6% of the time, Pallas kernels for 0%

commit v1 on v0

v1 whole, which is shorter than its diff:
```python
import functools
import math

import jax
import jax.numpy as jnp
from jax import lax
from jax.experimental import pallas as pl
from jax.experimental.pallas import tpu as pltpu
from jax.sharding import PartitionSpec as P

MESH = pl.DeviceIdType.MESH


def ring_order(count):
    outer = 4 if count % 4 == 0 else 1
    inner = count // outer
    if outer == 1 or inner == 1:
        return list(range(count))
    walk = [(0, 0)]
    for row in range(outer):
        columns = range(1, inner) if row % 2 == 0 else range(inner - 1, 0, -1)
        walk += [(row, column) for column in columns]
    walk += [(row, 0) for row in range(outer - 1, 0, -1)]
    return [row * inner + column for row, column in walk]


def decode_table(alive, data):
    nodes = [math.cos(math.pi * (j + 0.5) / data) for j in range(data)]
    lost = [1.0 - alive[j] for j in range(data)]
    lost_count = sum(lost)
    single = jnp.where(lost_count < 1.5, 1.0, 0.0)
    by_ones = single * alive[data]
    by_nodes = single * alive[data + 1]
    double = 1.0 - single
    table = []
    for j in range(data):
        row = [None] * (data + 2)
        gaps = [(b, double * lost[b]) for b in range(data) if b != j]
        for s in range(data):
            if s == j:
                row[s] = alive[j]
                continue
            value = -by_ones - by_nodes * (nodes[s] / nodes[j])
            for b, on in gaps:
                if b != s:
                    value = value + on * ((nodes[b] - nodes[s]) / (nodes[j] - nodes[b]))
            row[s] = lost[j] * alive[s] * value
        ones_value, nodes_value = by_ones, by_nodes * (1.0 / nodes[j])
        for b, on in gaps:
            ones_value = ones_value - on * (nodes[b] / (nodes[j] - nodes[b]))
            nodes_value = nodes_value + on * (1.0 / (nodes[j] - nodes[b]))
        row[data] = lost[j] * ones_value
        row[data + 1] = lost[j] * nodes_value
        table.append(row)
    return table


def kernel(
    codes, vocabs, order, subs,
    left_ref, x_ref, w_ref, out_ref,
    lat, wbuf, enc, rx, stat_tx, stat_rx,
    w_sem, x_sem, ring_send, ring_recv, pair_send, pair_recv, tx_sem, rx_sem, st_send, st_recv,
):
    me = lax.axis_index("code")
    v = lax.axis_index("vocab")
    batch, depth = x_ref.shape
    share_rows = w_ref.shape[1]
    rows = batch // codes
    phases = codes // 2
    data = left_ref.shape[1]
    half = vocabs // 2
    core = lax.rem(me, 2)
    sgn = 1 - 2 * core
    partner = me + sgn

    pos = jnp.int32(0)
    for i in range(vocabs):
        pos = pos + jnp.where(v == order[i], i, 0)

    def place(shift):
        return lax.rem(pos + shift + 2 * vocabs, vocabs)

    def device_at(where):
        found = jnp.int32(0)
        for i in range(vocabs):
            found = found + jnp.where(where == i, order[i], 0)
        return found

    ahead = device_at(place(sgn))
    behind = device_at(place(-sgn))

    for i in range(vocabs):
        pltpu.make_async_copy(
            w_ref.at[0, :, pl.ds(order[i] * depth, depth)], wbuf.at[i], w_sem.at[i]
        ).start()
    own_copy = pltpu.make_async_copy(x_ref, lat.at[pos], x_sem.at[0])
    own_copy.start()

    barrier = pltpu.get_barrier_semaphore()
    for k in range(1, codes):
        pl.semaphore_signal(barrier, inc=1, device_id={"code": lax.rem(me + k, codes)}, device_id_type=MESH)
    for k in range(1, vocabs):
        pl.semaphore_signal(barrier, inc=1, device_id={"vocab": lax.rem(v + k, vocabs)}, device_id_type=MESH)
    pl.semaphore_wait(barrier, codes + vocabs - 2)

    piece = rows // 2
    many = 2 // subs

    def piece_rows(phase, sub, which):
        start = (sub * phases + phase) * rows + which * piece
        return pl.ds(pl.multiple_of(start, 16), piece)

    def slot(phase, sub, way, d):
        return ((phase * 2 + sub) * 2 + way) * half + d - 1

    def ring_copy(phase, sub, way, d):
        source_place = place(-sgn * (d - 1)) if way == 0 else place(sgn * (d - 1))
        rs = piece_rows(phase, sub, core)
        src = x_ref.at[rs, :] if d == 1 else lat.at[source_place, rs, :]
        return pltpu.make_async_remote_copy(
            src_ref=src,
            dst_ref=lat.at[source_place, rs, :],
            send_sem=ring_send.at[slot(phase, sub, way, d)],
            recv_sem=ring_recv.at[slot(phase, sub, way, d)],
            device_id={"vocab": ahead if way == 0 else behind},
            device_id_type=MESH,
        )

    def arrival(phase, sub, way, d):
        source_place = place(-sgn * d) if way == 0 else place(sgn * d)
        rs = piece_rows(phase, sub, core)
        return pltpu.make_async_remote_copy(
            src_ref=lat.at[source_place, rs, :],
            dst_ref=lat.at[source_place, rs, :],
            send_sem=ring_send.at[slot(phase, sub, way, d)],
            recv_sem=ring_recv.at[slot(phase, sub, way, d)],
            device_id={"vocab": ahead if way == 0 else behind},
            device_id_type=MESH,
        )

    def pair_copy(phase, sub, way, d):
        source_place = place(-sgn * d) if way == 0 else place(sgn * d)
        rs = piece_rows(phase, sub, core)
        return pltpu.make_async_remote_copy(
            src_ref=lat.at[source_place, rs, :],
            dst_ref=lat.at[source_place, rs, :],
            send_sem=pair_send.at[slot(phase, sub, way, d)],
            recv_sem=pair_recv.at[slot(phase, sub, way, d)],
            device_id={"code": partner},
            device_id_type=MESH,
        )

    def pair_arrival(phase, sub, way, d):
        source_place = place(sgn * d) if way == 0 else place(-sgn * d)
        rs = piece_rows(phase, sub, 1 - core)
        return pltpu.make_async_remote_copy(
            src_ref=lat.at[source_place, rs, :],
            dst_ref=lat.at[source_place, rs, :],
            send_sem=pair_send.at[slot(phase, sub, way, d)],
            recv_sem=pair_recv.at[slot(phase, sub, way, d)],
            device_id={"code": partner},
            device_id_type=MESH,
        )

    def reach(way):
        return half if way == 0 else half - 1

    sends = []

    def begin(phase):
        for sub in range(2):
            for way in range(2):
                if reach(way) >= 1:
                    copy = ring_copy(phase, sub, way, 1)
                    copy.start()
                    sends.append(copy)

    def multiply(phase, where, first):
        for sub in range(2):
            block = sub * phases + phase
            part = lax.dot_general(
                lat[where, pl.ds(block * rows, rows), :],
                wbuf[where],
                (((1,), (1,)), ((), ())),
                preferred_element_type=jnp.float32,
            )
            enc[block] = part if first else enc[block] + part

    def take(phase, d):
        for sub in range(2):
            for way in range(2):
                if d <= reach(way):
                    pair_arrival(phase, sub, way, d).wait_recv()
        multiply(phase, place(-sgn * d), False)
        if d < half:
            multiply(phase, place(sgn * d), False)

    begin(0)
    own_copy.wait()
    for i in range(vocabs):
        pltpu.make_async_copy(
            w_ref.at[0, :, pl.ds(order[i] * depth, depth)], wbuf.at[i], w_sem.at[i]
        ).wait()

    for phase in range(phases):
        multiply(phase, pos, True)
        for d in range(1, half + 1):
            for sub in range(2):
                for way in range(2):
                    if d > reach(way):
                        continue
                    arrival(phase, sub, way, d).wait_recv()
                    if d < reach(way):
                        onward = ring_copy(phase, sub, way, d + 1)
                        onward.start()
                        sends.append(onward)
                    across = pair_copy(phase, sub, way, d)
                    across.start()
                    sends.append(across)
            if d == max(half - 1, 1) and phase + 1 < phases:
                begin(phase + 1)
            if d > 1:
                take(phase, d - 1)
        take(phase, half)
        for sub in range(2):
            block = sub * phases + phase

            @pl.when(me != block)
            def _():
                pltpu.make_async_remote_copy(
                    src_ref=enc.at[block],
                    dst_ref=rx.at[me],
                    send_sem=tx_sem.at[block],
                    recv_sem=rx_sem.at[me],
                    device_id={"code": jnp.int32(block)},
                    device_id_type=MESH,
                ).start()

    rx[me] = enc[me]

    alive = []
    for s in range(codes):
        here = jnp.int32(0)
        for k in range(data):
            here = here + jnp.where(left_ref[0, k] == s, 1, 0)
        alive.append(here.astype(jnp.float32))
    table = decode_table(alive, data)

    for k in range(1, codes):
        other = lax.rem(me + k, codes)
        pltpu.make_async_remote_copy(
            src_ref=enc.at[0],
            dst_ref=rx.at[other],
            send_sem=tx_sem.at[other],
            recv_sem=rx_sem.at[other],
            device_id={"code": other},
            device_id_type=MESH,
        ).wait_recv()

    top = None
    logits = []
    for j in range(data):
        value = table[j][0] * rx[0]
        for s in range(1, codes):
            value = value + table[j][s] * rx[s]
        logits.append(value)
        out_ref[:, j * share_rows:(j + 1) * share_rows] = value
        peak = jnp.max(value, axis=1, keepdims=True)
        top = peak if top is None else jnp.maximum(top, peak)
    total = None
    for j in range(data):
        part = jnp.sum(jnp.exp(logits[j] - top), axis=1, keepdims=True)
        total = part if total is None else total + part

    lane = lax.broadcasted_iota(jnp.int32, (rows, 128), 1)
    both = jnp.where(lane == 0, top, total)
    stat_tx[...] = jnp.transpose(both)[:8, :]
    stat_rx[v] = stat_tx[...]
    stat_sends = []
    for k in range(1, vocabs):
        copy = pltpu.make_async_remote_copy(
            src_ref=stat_tx,
            dst_ref=stat_rx.at[v],
            send_sem=st_send.at[k],
            recv_sem=st_recv.at[v],
            device_id={"vocab": lax.rem(v + k, vocabs)},
            device_id_type=MESH,
        )
        copy.start()
        stat_sends.append(copy)
    for copy in sends:
        copy.wait_send()
    for k in range(1, codes):
        other = lax.rem(me + k, codes)
        pltpu.make_async_remote_copy(
            src_ref=enc.at[0],
            dst_ref=rx.at[other],
            send_sem=tx_sem.at[other],
            recv_sem=rx_sem.at[other],
            device_id={"code": other},
            device_id_type=MESH,
        ).wait_send()
    for k in range(1, vocabs):
        other = lax.rem(v + k, vocabs)
        pltpu.make_async_remote_copy(
            src_ref=stat_tx,
            dst_ref=stat_rx.at[other],
            send_sem=st_send.at[k],
            recv_sem=st_recv.at[other],
            device_id={"vocab": other},
            device_id_type=MESH,
        ).wait_recv()

    stats = stat_rx[...]
    tops, totals = stats[:, 0:1, :], stats[:, 1:2, :]
    peak = jnp.max(tops, axis=0)
    whole = jnp.sum(totals * jnp.exp(tops - peak[None]), axis=0)
    normalizer = jnp.transpose(jnp.broadcast_to(peak + jnp.log(whole), (128, rows)))[:, 0:1]
    out_ref[...] = out_ref[...] - normalizer
    for copy in stat_sends:
        copy.wait_send()


def solution(mesh):
    codes, vocabs = mesh.shape["code"], mesh.shape["vocab"]
    order = ring_order(vocabs)

    def shards(latent_activations, code_fragments, remaining_fragments):
        batch, depth = latent_activations.shape
        share_rows = code_fragments.shape[1]
        data = remaining_fragments.shape[1]
        rows = batch // codes
        slots = (codes // 2) * 2 * 2 * (vocabs // 2)
        dma = pltpu.SemaphoreType.DMA
        return pl.pallas_call(
            functools.partial(kernel, codes, vocabs, order, 1),
            out_shape=jax.ShapeDtypeStruct((rows, data * share_rows), jnp.float32),
            in_specs=[
                pl.BlockSpec(memory_space=pltpu.SMEM),
                pl.BlockSpec(memory_space=pl.ANY),
                pl.BlockSpec(memory_space=pl.ANY),
            ],
            out_specs=pl.BlockSpec(memory_space=pltpu.VMEM),
            scratch_shapes=[
                pltpu.VMEM((vocabs, batch, depth), jnp.bfloat16),
                pltpu.VMEM((vocabs, share_rows, depth), jnp.bfloat16),
                pltpu.VMEM((codes, rows, share_rows), jnp.float32),
                pltpu.VMEM((codes, rows, share_rows), jnp.float32),
                pltpu.VMEM((8, rows), jnp.float32),
                pltpu.VMEM((vocabs, 8, rows), jnp.float32),
                dma((vocabs,)),
                dma((1,)),
                dma((slots,)),
                dma((slots,)),
                dma((slots,)),
                dma((slots,)),
                dma((codes,)),
                dma((codes,)),
                dma((vocabs,)),
                dma((vocabs,)),
            ],
            compiler_params=pltpu.CompilerParams(collective_id=0, has_side_effects=True),
        )(remaining_fragments, latent_activations, code_fragments)

    return jax.shard_map(
        shards,
        mesh=mesh,
        in_specs=(P(None, "vocab"), P("code", "vocab", None), P("vocab", None)),
        out_specs=P("code", "vocab"),
        check_vma=False,
    )
```

time: 218 us -> 72.7 us (0.33)
  the two profiles are of different devices: /device:TPU:0 before, /device:TPU:1 now
where the time goes in v1:
time: 72.7 us; the launch traced here: 72.5 us
  Pallas kernels  70.3 us (97%)
  local copies, waits for them, and re-layouts  2.21 us (3%)
    pallas_call x1, Pallas kernels, shards(): pl.pallas_call(functools.partial(kernel, codes, vocabs, order, 1), out_sh...  70.3 us
    pallas_call x1, local copies, waits for them, and re-layouts, shards(): pl.pallas_call(functools.partial(kernel, codes, vocabs, order, 1), out_sh...  2.21 us

profile of v1, /device:TPU:1, one launch (start us, length us, event | category | flops | bytes accessed | tf_op | source)
XLA Modules:
  0.0 72.5 jit_solution(2122084387497999282)
XLA Ops:
  0.0 70.3 %shard_map.37 = f32[128,1336]{1,0:T(8,128)} custom-call(s32[1,2]{1,0:T(1,128)} %left_ref.1, bf16[512,1024]{1,0:T(8,128)(2,1)} %x_ref.1, bf16[1,668,8192]{2,1,0:T(8,128)(2,1)} %w_ref.1), custom_call_target="tpu_custom_call" | custom-call | tf_op jit(solution)/shard_map/pallas_call | solution.py:335
  70.3 2.2 %copy.4 = f32[128,1336]{0,1:T(8,128)} copy(f32[128,1336]{1,0:T(8,128)} %shard_map.37) | data formatting | bytes 1368064 | tf_op jit(solution)/shard_map/pallas_call | solution.py:335

commit v2 on v1

--- a/solution.py
+++ b/solution.py
@@ -99,9 +99,9 @@
     barrier = pltpu.get_barrier_semaphore()
     for k in range(1, codes):
         pl.semaphore_signal(barrier, inc=1, device_id={"code": lax.rem(me + k, codes)}, device_id_type=MESH)
-    for k in range(1, vocabs):
-        pl.semaphore_signal(barrier, inc=1, device_id={"vocab": lax.rem(v + k, vocabs)}, device_id_type=MESH)
-    pl.semaphore_wait(barrier, codes + vocabs - 2)
+    for neighbour in (ahead, behind):
+        pl.semaphore_signal(barrier, inc=1, device_id={"vocab": neighbour}, device_id_type=MESH)
+    pl.semaphore_wait(barrier, codes + 1)
 
     piece = rows // 2
     many = 2 // subs
@@ -176,15 +176,17 @@
                     sends.append(copy)
 
     def multiply(phase, where, first):
+        hidden = [lat[where, pl.ds((sub * phases + phase) * rows, rows), :] for sub in range(2)]
+        part = lax.dot_general(
+            wbuf[where],
+            jnp.concatenate(hidden, axis=0),
+            (((1,), (1,)), ((), ())),
+            preferred_element_type=jnp.float32,
+        )
         for sub in range(2):
             block = sub * phases + phase
-            part = lax.dot_general(
-                lat[where, pl.ds(block * rows, rows), :],
-                wbuf[where],
-                (((1,), (1,)), ((), ())),
-                preferred_element_type=jnp.float32,
-            )
-            enc[block] = part if first else enc[block] + part
+            mine = part[:, sub * rows:(sub + 1) * rows]
+            enc[block] = mine if first else enc[block] + mine
 
     def take(phase, d):
         for sub in range(2):
@@ -264,17 +266,16 @@
         for s in range(1, codes):
             value = value + table[j][s] * rx[s]
         logits.append(value)
-        out_ref[:, j * share_rows:(j + 1) * share_rows] = value
-        peak = jnp.max(value, axis=1, keepdims=True)
+        out_ref[j * share_rows:(j + 1) * share_rows, :] = value
+        peak = jnp.max(value, axis=0, keepdims=True)
         top = peak if top is None else jnp.maximum(top, peak)
     total = None
     for j in range(data):
-        part = jnp.sum(jnp.exp(logits[j] - top), axis=1, keepdims=True)
+        part = jnp.sum(jnp.exp(logits[j] - top), axis=0, keepdims=True)
         total = part if total is None else total + part
 
-    lane = lax.broadcasted_iota(jnp.int32, (rows, 128), 1)
-    both = jnp.where(lane == 0, top, total)
-    stat_tx[...] = jnp.transpose(both)[:8, :]
+    line = lax.broadcasted_iota(jnp.int32, (8, rows), 0)
+    stat_tx[...] = jnp.where(line == 0, top, total)
     stat_rx[v] = stat_tx[...]
     stat_sends = []
     for k in range(1, vocabs):
@@ -315,8 +316,7 @@
     tops, totals = stats[:, 0:1, :], stats[:, 1:2, :]
     peak = jnp.max(tops, axis=0)
     whole = jnp.sum(totals * jnp.exp(tops - peak[None]), axis=0)
-    normalizer = jnp.transpose(jnp.broadcast_to(peak + jnp.log(whole), (128, rows)))[:, 0:1]
-    out_ref[...] = out_ref[...] - normalizer
+    out_ref[...] = out_ref[...] - (peak + jnp.log(whole))
     for copy in stat_sends:
         copy.wait_send()
 
@@ -334,7 +334,7 @@
         dma = pltpu.SemaphoreType.DMA
         return pl.pallas_call(
             functools.partial(kernel, codes, vocabs, order, 1),
-            out_shape=jax.ShapeDtypeStruct((rows, data * share_rows), jnp.float32),
+            out_shape=jax.ShapeDtypeStruct((data * share_rows, rows), jnp.float32),
             in_specs=[
                 pl.BlockSpec(memory_space=pltpu.SMEM),
                 pl.BlockSpec(memory_space=pl.ANY),
@@ -344,8 +344,8 @@
             scratch_shapes=[
                 pltpu.VMEM((vocabs, batch, depth), jnp.bfloat16),
                 pltpu.VMEM((vocabs, share_rows, depth), jnp.bfloat16),
-                pltpu.VMEM((codes, rows, share_rows), jnp.float32),
-                pltpu.VMEM((codes, rows, share_rows), jnp.float32),
+                pltpu.VMEM((codes, share_rows, rows), jnp.float32),
+                pltpu.VMEM((codes, share_rows, rows), jnp.float32),
                 pltpu.VMEM((8, rows), jnp.float32),
                 pltpu.VMEM((vocabs, 8, rows), jnp.float32),
                 dma((vocabs,)),
@@ -360,7 +360,7 @@
                 dma((vocabs,)),
             ],
             compiler_params=pltpu.CompilerParams(collective_id=0, has_side_effects=True),
-        )(remaining_fragments, latent_activations, code_fragments)
+        )(remaining_fragments, latent_activations, code_fragments).T
 
     return jax.shard_map(
         shards,

time: 72.7 us -> 68.7 us (0.945)
  Pallas kernels: 70.3 us -> 66.6 us
    pallas_call x1, Pallas kernels: 70.3 us -> 66.6 us  [shards(): pl.pallas_call(functools.partial(kernel, codes, vocabs, order, 1), out_sh...]
    pallas_call x1 -> x0, local copies, waits for them, and re-layouts: 2.21 us -> none  [shards(): pl.pallas_call(functools.partial(kernel, codes, vocabs, order, 1), out_sh...]
    unnamed x0 -> x1, local copies, waits for them, and re-layouts: none -> 1.99 us
where the time goes in v2:
time: 68.7 us; the launch traced here: 68.6 us
  Pallas kernels  66.6 us (97%)
  local copies, waits for them, and re-layouts  1.99 us (3%)
    pallas_call x1, Pallas kernels, shards(): pl.pallas_call(functools.partial(kernel, codes, vocabs, order, 1), out_sh...  66.6 us
    unnamed x1, local copies, waits for them, and re-layouts  1.99 us

profile of v2, /device:TPU:1, one launch (start us, length us, event | category | flops | bytes accessed | tf_op | source)
XLA Modules:
  0.0 68.6 jit_solution(13932737285690153937)
XLA Ops:
  0.0 66.6 %shard_map.37 = f32[1336,128]{1,0:T(8,128)} custom-call(s32[1,2]{1,0:T(1,128)} %left_ref.1, bf16[512,1024]{1,0:T(8,128)(2,1)} %x_ref.1, bf16[1,668,8192]{2,1,0:T(8,128)(2,1)} %w_ref.1), custom_call_target="tpu_custom_call" | custom-call | tf_op jit(solution)/shard_map/pallas_call | solution.py:335
  66.6 2.0 %copy.5 = f32[128,1336]{0,1:T(8,128)} copy(f32[128,1336]{0,1:T(8,128)} %bitcast.1) | data formatting | bytes 1368064

commit v3 on v2

--- a/solution.py
+++ b/solution.py
@@ -9,6 +9,8 @@
 from jax.sharding import PartitionSpec as P
 
 MESH = pl.DeviceIdType.MESH
+
+SIDE_SHARE = 0.375
 
 
 def ring_order(count):
@@ -56,10 +58,11 @@
 
 
 def kernel(
-    codes, vocabs, order, subs,
+    codes, vocabs, order, width,
     left_ref, x_ref, w_ref, out_ref,
     lat, wbuf, enc, rx, stat_tx, stat_rx,
-    w_sem, x_sem, ring_send, ring_recv, pair_send, pair_recv, tx_sem, rx_sem, st_send, st_recv,
+    w_sem, x_sem, ring_send, ring_recv, pair_send, pair_recv,
+    side_send, side_recv, pass_send, pass_recv, tx_sem, rx_sem, st_send, st_recv,
 ):
     me = lax.axis_index("code")
     v = lax.axis_index("vocab")
@@ -72,6 +75,7 @@
     core = lax.rem(me, 2)
     sgn = 1 - 2 * core
     partner = me + sgn
+    across_y = lax.rem(me + 2, codes)
 
     pos = jnp.int32(0)
     for i in range(vocabs):
@@ -89,10 +93,6 @@
     ahead = device_at(place(sgn))
     behind = device_at(place(-sgn))
 
-    for i in range(vocabs):
-        pltpu.make_async_copy(
-            w_ref.at[0, :, pl.ds(order[i] * depth, depth)], wbuf.at[i], w_sem.at[i]
-        ).start()
     own_copy = pltpu.make_async_copy(x_ref, lat.at[pos], x_sem.at[0])
     own_copy.start()
 
@@ -104,63 +104,70 @@
     pl.semaphore_wait(barrier, codes + 1)
 
     piece = rows // 2
-    many = 2 // subs
+
+    def target(phase):
+        return lax.rem(me // 2 + 1 + phase, phases)
 
     def piece_rows(phase, sub, which):
-        start = (sub * phases + phase) * rows + which * piece
+        start = (2 * target(phase) + sub) * rows + which * piece
         return pl.ds(pl.multiple_of(start, 16), piece)
 
     def slot(phase, sub, way, d):
         return ((phase * 2 + sub) * 2 + way) * half + d - 1
 
+    def ring_columns(phase):
+        return pl.ds(width, depth - width) if phase == phases - 1 else pl.ds(0, depth)
+
+    side_columns = pl.ds(0, width)
+
+    def origin(way, d):
+        return place(-sgn * d) if way == 0 else place(sgn * d)
+
+    def move(src, dst, send, recv, device):
+        return pltpu.make_async_remote_copy(
+            src_ref=src, dst_ref=dst, send_sem=send, recv_sem=recv, device_id=device, device_id_type=MESH
+        )
+
     def ring_copy(phase, sub, way, d):
-        source_place = place(-sgn * (d - 1)) if way == 0 else place(sgn * (d - 1))
-        rs = piece_rows(phase, sub, core)
-        src = x_ref.at[rs, :] if d == 1 else lat.at[source_place, rs, :]
-        return pltpu.make_async_remote_copy(
-            src_ref=src,
-            dst_ref=lat.at[source_place, rs, :],
-            send_sem=ring_send.at[slot(phase, sub, way, d)],
-            recv_sem=ring_recv.at[slot(phase, sub, way, d)],
-            device_id={"vocab": ahead if way == 0 else behind},
-            device_id_type=MESH,
-        )
+        rs, cs, at = piece_rows(phase, sub, core), ring_columns(phase), slot(phase, sub, way, d)
+        dst = lat.at[origin(way, d - 1), rs, cs]
+        src = x_ref.at[rs, cs] if d == 1 else dst
+        return move(src, dst, ring_send.at[at], ring_recv.at[at], {"vocab": ahead if way == 0 else behind})
 
     def arrival(phase, sub, way, d):
-        source_place = place(-sgn * d) if way == 0 else place(sgn * d)
-        rs = piece_rows(phase, sub, core)
-        return pltpu.make_async_remote_copy(
-            src_ref=lat.at[source_place, rs, :],
-            dst_ref=lat.at[source_place, rs, :],
-            send_sem=ring_send.at[slot(phase, sub, way, d)],
-            recv_sem=ring_recv.at[slot(phase, sub, way, d)],
-            device_id={"vocab": ahead if way == 0 else behind},
-            device_id_type=MESH,
-        )
+        at = slot(phase, sub, way, d)
+        here = lat.at[origin(way, d), piece_rows(phase, sub, core), ring_columns(phase)]
+        return move(here, here, ring_send.at[at], ring_recv.at[at], {"vocab": ahead if way == 0 else behind})
 
     def pair_copy(phase, sub, way, d):
-        source_place = place(-sgn * d) if way == 0 else place(sgn * d)
-        rs = piece_rows(phase, sub, core)
-        return pltpu.make_async_remote_copy(
-            src_ref=lat.at[source_place, rs, :],
-            dst_ref=lat.at[source_place, rs, :],
-            send_sem=pair_send.at[slot(phase, sub, way, d)],
-            recv_sem=pair_recv.at[slot(phase, sub, way, d)],
-            device_id={"code": partner},
-            device_id_type=MESH,
-        )
+        at = slot(phase, sub, way, d)
+        here = lat.at[origin(way, d), piece_rows(phase, sub, core), ring_columns(phase)]
+        return move(here, here, pair_send.at[at], pair_recv.at[at], {"code": partner})
 
     def pair_arrival(phase, sub, way, d):
-        source_place = place(sgn * d) if way == 0 else place(-sgn * d)
-        rs = piece_rows(phase, sub, 1 - core)
-        return pltpu.make_async_remote_copy(
-            src_ref=lat.at[source_place, rs, :],
-            dst_ref=lat.at[source_place, rs, :],
-            send_sem=pair_send.at[slot(phase, sub, way, d)],
-            recv_sem=pair_recv.at[slot(phase, sub, way, d)],
-            device_id={"code": partner},
-            device_id_type=MESH,
-        )
+        at = slot(phase, sub, way, d)
+        here = lat.at[origin(1 - way, d), piece_rows(phase, sub, 1 - core), ring_columns(phase)]
+        return move(here, here, pair_send.at[at], pair_recv.at[at], {"code": partner})
+
+    def side_copy(sub, way, d):
+        at = slot(0, sub, way, d)
+        here = lat.at[origin(way, d), piece_rows(0, sub, core), side_columns]
+        return move(here, here, side_send.at[at], side_recv.at[at], {"code": across_y})
+
+    def side_arrival(sub, way, d):
+        at = slot(0, sub, way, d)
+        here = lat.at[origin(way, d), piece_rows(phases - 1, sub, core), side_columns]
+        return move(here, here, side_send.at[at], side_recv.at[at], {"code": across_y})
+
+    def pass_copy(sub, way, d):
+        at = slot(0, sub, way, d)
+        here = lat.at[origin(way, d), piece_rows(phases - 1, sub, core), side_columns]
+        return move(here, here, pass_send.at[at], pass_recv.at[at], {"code": partner})
+
+    def pass_arrival(sub, way, d):
+        at = slot(0, sub, way, d)
+        here = lat.at[origin(1 - way, d), piece_rows(phases - 1, sub, 1 - core), side_columns]
+        return move(here, here, pass_send.at[at], pass_recv.at[at], {"code": partner})
 
     def reach(way):
         return half if way == 0 else half - 1
@@ -176,15 +183,15 @@
                     sends.append(copy)
 
     def multiply(phase, where, first):
-        hidden = [lat[where, pl.ds((sub * phases + phase) * rows, rows), :] for sub in range(2)]
+        first_row = pl.multiple_of(2 * target(phase) * rows, 2 * rows)
         part = lax.dot_general(
             wbuf[where],
-            jnp.concatenate(hidden, axis=0),
+            lat[where, pl.ds(first_row, 2 * rows), :],
             (((1,), (1,)), ((), ())),
             preferred_element_type=jnp.float32,
         )
         for sub in range(2):
-            block = sub * phases + phase
+            block = 2 * target(phase) + sub
             mine = part[:, sub * rows:(sub + 1) * rows]
             enc[block] = mine if first else enc[block] + mine
 
@@ -193,50 +200,66 @@
             for way in range(2):
                 if d <= reach(way):
                     pair_arrival(phase, sub, way, d).wait_recv()
+                    if width and phase == phases - 1:
+                        pass_arrival(sub, way, d).wait_recv()
         multiply(phase, place(-sgn * d), False)
         if d < half:
             multiply(phase, place(sgn * d), False)
 
     begin(0)
-    own_copy.wait()
     for i in range(vocabs):
         pltpu.make_async_copy(
             w_ref.at[0, :, pl.ds(order[i] * depth, depth)], wbuf.at[i], w_sem.at[i]
-        ).wait()
-
-    for phase in range(phases):
-        multiply(phase, pos, True)
-        for d in range(1, half + 1):
-            for sub in range(2):
-                for way in range(2):
-                    if d > reach(way):
-                        continue
-                    arrival(phase, sub, way, d).wait_recv()
-                    if d < reach(way):
-                        onward = ring_copy(phase, sub, way, d + 1)
-                        onward.start()
-                        sends.append(onward)
-                    across = pair_copy(phase, sub, way, d)
-                    across.start()
-                    sends.append(across)
-            if d == max(half - 1, 1) and phase + 1 < phases:
-                begin(phase + 1)
-            if d > 1:
-                take(phase, d - 1)
-        take(phase, half)
-        for sub in range(2):
-            block = sub * phases + phase
-
-            @pl.when(me != block)
-            def _():
-                pltpu.make_async_remote_copy(
-                    src_ref=enc.at[block],
-                    dst_ref=rx.at[me],
-                    send_sem=tx_sem.at[block],
-                    recv_sem=rx_sem.at[me],
-                    device_id={"code": jnp.int32(block)},
-                    device_id_type=MESH,
-                ).start()
+        ).start()
+
+    def pieces(d):
+        return [(sub, way) for sub in range(2) for way in range(2) if d <= reach(way)]
+
+    def receive(phase, d):
+        for sub, way in pieces(d):
+            arrival(phase, sub, way, d).wait_recv()
+            copies = [ring_copy(phase, sub, way, d + 1)] if d < reach(way) else []
+            copies.append(pair_copy(phase, sub, way, d))
+            if width and phase == 0:
+                copies.append(side_copy(sub, way, d))
+            for copy in copies:
+                copy.start()
+                sends.append(copy)
+        if d == max(half - 1, 1) and phase + 1 < phases:
+            begin(phase + 1)
+
+    def hand_on(phase, d):
+        if width and phase == 0:
+            for sub, way in pieces(d):
+                side_arrival(sub, way, d).wait_recv()
+                copy = pass_copy(sub, way, d)
+                copy.start()
+                sends.append(copy)
+
+    def deliver(phase):
+        there = 2 * target(phase)
+        for block in (there, there + 1) if phase < phases - 1 else (partner,):
+            move(enc.at[block], rx.at[me], tx_sem.at[block], rx_sem.at[me], {"code": block}).start()
+
+    steps = [(phase, d) for phase in range(phases) for d in range(1, half + 1)]
+    for t in range(len(steps) + 2):
+        if t < len(steps):
+            receive(*steps[t])
+        if 1 <= t <= len(steps):
+            hand_on(*steps[t - 1])
+        if t == 2:
+            own_copy.wait()
+            for i in range(vocabs):
+                pltpu.make_async_copy(
+                    w_ref.at[0, :, pl.ds(order[i] * depth, depth)], wbuf.at[i], w_sem.at[i]
+                ).wait()
+        if t >= 2:
+            phase, d = steps[t - 2]
+            if d == 1:
+                multiply(phase, pos, True)
+            take(phase, d)
+            if d == half:
+                deliver(phase)
 
     rx[me] = enc[me]
 
@@ -330,10 +353,11 @@
         share_rows = code_fragments.shape[1]
         data = remaining_fragments.shape[1]
         rows = batch // codes
+        width = int(depth * SIDE_SHARE) // 128 * 128 if codes == 4 else 0
         slots = (codes // 2) * 2 * 2 * (vocabs // 2)
         dma = pltpu.SemaphoreType.DMA
         return pl.pallas_call(
-            functools.partial(kernel, codes, vocabs, order, 1),
+            functools.partial(kernel, codes, vocabs, order, width),
             out_shape=jax.ShapeDtypeStruct((data * share_rows, rows), jnp.float32),
             in_specs=[
                 pl.BlockSpec(memory_space=pltpu.SMEM),
@@ -350,10 +374,7 @@
                 pltpu.VMEM((vocabs, 8, rows), jnp.float32),
                 dma((vocabs,)),
                 dma((1,)),
-                dma((slots,)),
-                dma((slots,)),
-                dma((slots,)),
-                dma((slots,)),
+                *[dma((slots,)) for _ in range(8)],
                 dma((codes,)),
                 dma((codes,)),
                 dma((vocabs,)),

time: 68.7 us -> 60.1 us (0.87)
  Pallas kernels: 66.6 us -> 57.9 us
    pallas_call x1, Pallas kernels: 66.6 us -> 57.9 us  [shards(): pl.pallas_call(functools.partial(kernel, codes, vocabs, order, width), ou...]
where the time goes in v3:
time: 60.1 us; the launch traced here: 59.9 us
  Pallas kernels  57.9 us (96%)
  local copies, waits for them, and re-layouts  1.99 us (3%)
    pallas_call x1, Pallas kernels, shards(): pl.pallas_call(functools.partial(kernel, codes, vocabs, order, width), ou...  57.9 us
    unnamed x1, local copies, waits for them, and re-layouts  1.99 us

profile of v3, /device:TPU:1, one launch (start us, length us, event | category | flops | bytes accessed | tf_op | source)
XLA Modules:
  0.0 59.9 jit_solution(11818510741095461640)
XLA Ops:
  0.0 57.9 %shard_map.37 = f32[1336,128]{1,0:T(8,128)} custom-call(s32[1,2]{1,0:T(1,128)} %left_ref.1, bf16[512,1024]{1,0:T(8,128)(2,1)} %x_ref.1, bf16[1,668,8192]{2,1,0:T(8,128)(2,1)} %w_ref.1), custom_call_target="tpu_custom_call" | custom-call | tf_op jit(solution)/shard_map/pallas_call | solution.py:359
  57.9 2.0 %copy.5 = f32[128,1336]{0,1:T(8,128)} copy(f32[128,1336]{0,1:T(8,128)} %bitcast.1) | data formatting | bytes 1368064

commit v4 on v3

--- a/solution.py
+++ b/solution.py
@@ -10,7 +10,7 @@
 
 MESH = pl.DeviceIdType.MESH
 
-SIDE_SHARE = 0.375
+SIDE_SHARE = 0.5
 
 
 def ring_order(count):
@@ -242,24 +242,27 @@
             move(enc.at[block], rx.at[me], tx_sem.at[block], rx_sem.at[me], {"code": block}).start()
 
     steps = [(phase, d) for phase in range(phases) for d in range(1, half + 1)]
-    for t in range(len(steps) + 2):
-        if t < len(steps):
-            receive(*steps[t])
-        if 1 <= t <= len(steps):
-            hand_on(*steps[t - 1])
-        if t == 2:
+    for t, (phase, d) in enumerate(steps):
+        receive(phase, d)
+        if t == min(1, half - 1):
             own_copy.wait()
             for i in range(vocabs):
                 pltpu.make_async_copy(
                     w_ref.at[0, :, pl.ds(order[i] * depth, depth)], wbuf.at[i], w_sem.at[i]
                 ).wait()
-        if t >= 2:
-            phase, d = steps[t - 2]
+        if d > 1:
+            if d == 2:
+                multiply(phase, pos, True)
+            take(phase, d - 1)
+        if d == half:
             if d == 1:
                 multiply(phase, pos, True)
             take(phase, d)
-            if d == half:
-                deliver(phase)
+            deliver(phase)
+        if d > 1:
+            hand_on(phase, d - 1)
+        if d == half:
+            hand_on(phase, d)
 
     rx[me] = enc[me]
 

time: 60.1 us -> 56.5 us (0.940)
  Pallas kernels: 57.9 us -> 54.2 us
    pallas_call x1, Pallas kernels: 57.9 us -> 54.2 us  [shards(): pl.pallas_call(functools.partial(kernel, codes, vocabs, order, width), ou...]
where the time goes in v4:
time: 56.5 us; the launch traced here: 56.2 us
  Pallas kernels  54.2 us (96%)
  local copies, waits for them, and re-layouts  1.99 us (4%)
    pallas_call x1, Pallas kernels, shards(): pl.pallas_call(functools.partial(kernel, codes, vocabs, order, width), ou...  54.2 us
    unnamed x1, local copies, waits for them, and re-layouts  1.99 us

profile of v4, /device:TPU:1, one launch (start us, length us, event | category | flops | bytes accessed | tf_op | source)
XLA Modules:
  0.0 56.2 jit_solution(9653442453820226986)
XLA Ops:
  0.0 54.2 %shard_map.37 = f32[1336,128]{1,0:T(8,128)} custom-call(s32[1,2]{1,0:T(1,128)} %left_ref.1, bf16[512,1024]{1,0:T(8,128)(2,1)} %x_ref.1, bf16[1,668,8192]{2,1,0:T(8,128)(2,1)} %w_ref.1), custom_call_target="tpu_custom_call" | custom-call | tf_op jit(solution)/shard_map/pallas_call | solution.py:362
  54.2 2.0 %copy.5 = f32[128,1336]{0,1:T(8,128)} copy(f32[128,1336]{0,1:T(8,128)} %bitcast.1) | data formatting | bytes 1368064
